TPU v7x, 32 devices: a whole 2x2x4 slice. The times are simulated.
32 devices in a mesh: gx: 4 (over z), gy: 8 (over y, x, core).
Axes of the slice: x: 2, y: 2, z: 4, core: 2. Of those that a mesh axis runs over, the one named last changes fastest.
Arguments:
- operator_blocks: bfloat16 [256, 6, 256, 256], P(('gx', 'gy')), may hold values from -0.15625 to 0.15625
- local_columns: int32 [256, 2], P(('gx', 'gy')), may hold values from 0 to 7
- remote_columns: int32 [256, 4], P(('gx', 'gy')), may hold values from 8 to 17
- match_slots: int32 [256, 6, 2], P(('gx', 'gy')), may hold values from 0 to 2
- tentative: bfloat16 [256, 2, 256, 256], P(('gx', 'gy')), may hold values from -1.5 to 1.5
- inverse_diagonal: bfloat16 [256, 256, 256], P(('gx', 'gy')), may hold values from -0.375 to 0.375
- peer_sends: int32 [32, 8], P(('gx', 'gy')), may hold values from 0 to 7
- slab_sends: int32 [32, 2], P(('gx', 'gy')), may hold values from 0 to 7
- coarse_slots: int32 [256, 2, 2], P(('gx', 'gy')), may hold values from 0 to 47, as said below
Outputs:
- smoothed: bfloat16 [256, 2, 256, 256], P(('gx', 'gy'))
- coarse_operator: bfloat16 [192, 256, 256], P(('gx', 'gy'))
Inputs may be any that keep to these rules, and one draw needn't show every extreme that they name: `match_slots`: the value 2 stands for no matching block. `coarse_slots`: no two partial blocks of one device name the same coarse block; coarse block c of a slab belongs to the device of gy index c // 6.
All inputs are finite; a program needn't handle non-finite values.
Results may differ from a plain program's by a relative error of at most 0.012.
Values may be sent and summed in bfloat16 or wider, within the bound.
A program may use at most 128 MiB of HBM per device.

v0:
```python
import jax
import jax.numpy as jnp
from jax import lax
from jax.sharding import PartitionSpec as P

KL = 2
KP = 2
H = 1


def from_behind(value, axis, steps):
    count = lax.axis_size(axis)
    leading, last = (max(0, -steps), min(count, count - steps))
    return lax.ppermute(value, axis, [(source, source + steps) for source in range(leading, last)])


def select_blocks(picked, matches):
    selected = []
    for out_block in range(matches.shape[2]):
        chosen = jnp.zeros_like(picked[:, :, 0])
        for in_block in range(picked.shape[2]):
            matched = (matches[:, :, out_block] == in_block)[:, :, None, None]
            chosen = jnp.where(matched, picked[:, :, in_block], chosen)
        selected.append(chosen)
    return jnp.stack(selected, axis=2)


def block_product(blocks, lookup, columns, matches):
    chosen = select_blocks(lookup[columns], matches)
    return jnp.einsum("rkab,rknbc->rnac", blocks, chosen, preferred_element_type=jnp.float32)


def fetch_remote(fine_rows, peer_list, slab_list):
    outgoing = fine_rows[peer_list]
    from_peers = lax.all_to_all(outgoing, "gy", split_axis=0, concat_axis=0, tiled=True)
    from_below = from_behind(fine_rows[slab_list[:H]], "gx", 1)
    from_above = from_behind(fine_rows[slab_list[H:]], "gx", -1)
    return jnp.concatenate([from_peers, from_below, from_above], axis=0)


def apply_operator(
    operator_blocks, fine_rows, local_columns, remote_columns, match_slots, peer_list, slab_list
):
    local_part = block_product(
        operator_blocks[:, :KL], fine_rows, local_columns, match_slots[:, :KL]
    )
    remote = fetch_remote(fine_rows, peer_list, slab_list)
    remote_part = block_product(
        operator_blocks[:, KL:], remote, remote_columns - fine_rows.shape[0], match_slots[:, KL:]
    )
    return local_part + remote_part


def body(
    operator_blocks,
    local_columns,
    remote_columns,
    match_slots,
    tentative,
    inverse_diagonal,
    peer_sends,
    slab_sends,
    coarse_slots,
):
    peer_list = peer_sends.reshape(-1)
    slab_list = slab_sends.reshape(-1)
    width = tentative.shape[-1]
    group_size = lax.axis_size("gy")
    owned_slots = (3 * tentative.shape[0] * KP * KP // 2 + group_size - 1) // group_size
    fine_rows = tentative
    for smooth_pass in range(2):
        product = apply_operator(
            operator_blocks,
            fine_rows,
            local_columns,
            remote_columns,
            match_slots,
            peer_list,
            slab_list,
        )
        image = product.astype(jnp.bfloat16)
        update = jnp.einsum(
            "rab,rnbc->rnac", inverse_diagonal, image, preferred_element_type=jnp.float32
        )
        fine_rows = (fine_rows.astype(jnp.float32) - update).astype(jnp.bfloat16)
    final_image = apply_operator(
        operator_blocks, fine_rows, local_columns, remote_columns, match_slots, peer_list, slab_list
    ).astype(jnp.bfloat16)
    partial_value = jnp.einsum(
        "rnab,rmac->rnmbc", fine_rows, final_image, preferred_element_type=jnp.float32
    )
    partial_value = partial_value.astype(jnp.bfloat16).reshape(-1, width, width)
    slot_blocks = (
        jnp.zeros((group_size * owned_slots, width, width), jnp.bfloat16)
        .at[coarse_slots.reshape(-1)]
        .set(partial_value)
    )
    received = lax.all_to_all(slot_blocks, "gy", split_axis=0, concat_axis=0, tiled=True)
    coarse = jnp.sum(
        received.reshape(group_size, owned_slots, width, width), axis=0, dtype=jnp.float32
    )
    return (fine_rows, coarse.astype(jnp.bfloat16))


def solution(mesh):
    placed = (
        P(("gx", "gy"), None, None, None),
        P(("gx", "gy"), None),
        P(("gx", "gy"), None),
        P(("gx", "gy"), None, None),
        P(("gx", "gy"), None, None, None),
        P(("gx", "gy"), None, None),
        P(("gx", "gy"), None),
        P(("gx", "gy"), None),
        P(("gx", "gy"), None, None),
    )
    return jax.shard_map(
        body,
        mesh=mesh,
        in_specs=placed,
        out_specs=(P(("gx", "gy"), None, None, None), P(("gx", "gy"), None, None)),
        check_vma=False,
    )
```

profile of v0, /device:TPU:0, one launch (start us, length us, event | category | flops | bytes accessed | tf_op | source)
XLA Modules:
  0.0 310.1 jit_solution(14050203975187784053)
XLA Ops:
  0.6 1.3 fusion.88
  5.9 1.9 constant_dynamic-slice_fusion.5
  7.7 5.0 %collective-permute-start = (bf16[1,2,256,256]{3,2,1,0:T(8,128)(2,1)}, bf16[1,2,256,256]{3,2,1,0:T(8,128)(2,1)S(1)}, u32[]{:S(2)}, u32[]{:S(2)}) collective-permute-start(bf16[1,2,256,256]{3,2,1,0:T(8,128)(2,1)} %get-tuple-element.96), channel_id=1, source_target_pairs={{0,8},{8,16},{16,24},{1,9},{9,17},{17,25},{2,10},{10,18},{18,26},{... | collective-permute-start | bytes 786440 | tf_op jit(solution)/shard_map/ppermute | solution.py:14
  12.7 1.3 collective-permute-start.1
  14.0 0.7 fusion.75
  14.7 3.8 %gather_fusion.1 = bf16[8,2,256,256]{3,2,1,0:T(8,128)(2,1)} fusion(bf16[8,2,256,256]{3,2,1,0:T(8,128)(2,1)} %param.13, s32[1024]{0:T(1024)S(1)} %pad_clamp_fusion.1), kind=kCustom, calls=%fused_computation.1 | custom fusion | bytes 4194336 | tf_op jit(solution)/shard_map/gather | solution.py:34
  18.5 4.5 %all-to-all-start = ((bf16[8,2,256,256]{3,2,1,0:T(8,128)(2,1)}), bf16[8,2,256,256]{3,2,1,0:T(8,128)(2,1)}, u32[]{:S(2)}, u32[]{:S(2)}) async-start(bf16[8,2,256,256]{3,2,1,0:T(8,128)(2,1)} %gather_fusion.1), calls=%async_computation | async-start | bytes 4194304 | tf_op jit(solution)/shard_map/all_to_all | solution.py:35
  23.0 2.4 copy.63
  25.6 0.1 copy.105
  25.7 0.1 copy.106
  25.8 0.1 copy.107
  25.9 0.1 copy.108
  26.2 2.8 gather_fusion
  28.9 4.7 %fusion.87 = (bf16[8,2,1,256,256]{4,3,2,1,0:T(8,128)(2,1)}, bf16[8,2,1,256,256]{4,3,2,1,0:T(8,128)(2,1)}) fusion(bf16[8,2,2,256,256]{4,3,2,1,0:T(8,128)(2,1)} %bitcast.195), kind=kLoop, calls=%fused_computation.116 | loop fusion | bytes 8388608 | tf_op jit(solution)/shard_map/slice | solution.py:23
  33.6 2.8 copy.123
  36.4 3.9 %copy.124 = bf16[8,2,1,256,256]{3,4,1,2,0:T(8,128)(2,1)} copy(bf16[8,2,1,256,256]{4,3,2,1,0:T(8,128)(2,1)} %get-tuple-element.90) | data formatting | bytes 4194304
  40.4 4.0 %select_select_fusion.11 = (bf16[8,2,1,256,256]{3,4,1,2,0:T(8,128)(2,1)}, bf16[8,2,1,256,256]{3,4,1,2,0:T(8,128)(2,1)}) fusion(bf16[8,2,1,256,256]{3,4,1,2,0:T(8,128)(2,1)S(1)} %copy.123, bf16[8,2,1,256,256]{3,4,1,2,0:T(8,128)(2,1)} %copy.124, pred[8,2]{1,0:T(8,128)(4,1)S(1)} %bitcast.213, pred[8,2]{1,0:T(8,128)(4,1)S(1)} %bitcast.210, ...), kind=kLoop, calls=%fused_computation.80 | loop fusion | flops 4194304 | bytes 8388672 | tf_op jit(solution)/shard_map/jit(_where)/select_n | solution.py:23
  44.3 0.1 copy.110
  44.4 0.1 copy.111
  44.5 0.1 copy.112
  44.6 0.1 copy.109
  44.7 4.9 %all-to-all-done = bf16[8,2,256,256]{3,2,1,0:T(8,128)(2,1)} async-done(((bf16[8,2,256,256]{3,2,1,0:T(8,128)(2,1)}), bf16[8,2,256,256]{3,2,1,0:T(8,128)(2,1)}, u32[]{:S(2)}, u32[]{:S(2)}) %all-to-all-start) | async-done | bytes 2097184 | tf_op jit(solution)/shard_map/all_to_all | solution.py:35
  49.6 3.6 %pad_maximum_fusion = bf16[10,2,256,256]{3,2,1,0:T(8,128)(2,1)} fusion(bf16[1,2,256,256]{3,2,1,0:T(8,128)(2,1)} %collective-permute-done.1, bf16[1,2,256,256]{3,2,1,0:T(8,128)(2,1)S(1)} %collective-permute-done, bf16[8,2,256,256]{3,2,1,0:T(8,128)(2,1)} %all-to-all-done), kind=kLoop, calls=%fused_computation.61 | loop fusion | flops 2621440 | bytes 5242880 | tf_op jit(solution)/shard_map/concatenate | solution.py:38
  53.2 6.8 %gather_fusion.2 = bf16[32,2,256,256]{3,2,1,0:T(8,128)(2,1)} fusion(bf16[10,2,256,256]{3,2,1,0:T(8,128)(2,1)} %pad_maximum_fusion, s32[1024]{0:T(1024)S(1)} %pad_clamp_fusion), kind=kCustom, calls=%fused_computation.2 | custom fusion | bytes 16777344 | tf_op jit(solution)/shard_map/gather | solution.py:29
  60.0 5.9 %fusion.86 = (bf16[8,4,1,256,256]{4,3,2,1,0:T(8,128)(2,1)}, bf16[8,4,1,256,256]{4,3,2,1,0:T(8,128)(2,1)}) fusion(bf16[8,4,2,256,256]{4,3,2,1,0:T(8,128)(2,1)} %bitcast.193), kind=kLoop, calls=%fused_computation.115 | loop fusion | bytes 16777216 | tf_op jit(solution)/shard_map/slice | solution.py:23
  65.9 6.5 %copy.125 = bf16[8,4,1,256,256]{3,4,1,2,0:T(8,128)(2,1)} copy(bf16[8,4,1,256,256]{4,3,2,1,0:T(8,128)(2,1)} %get-tuple-element.83) | data formatting | bytes 8388608
  72.3 6.5 %copy.126 = bf16[8,4,1,256,256]{3,4,1,2,0:T(8,128)(2,1)} copy(bf16[8,4,1,256,256]{4,3,2,1,0:T(8,128)(2,1)} %get-tuple-element.82) | data formatting | bytes 8388608
  78.8 3.9 %select_select_fusion.5 = (bf16[8,4,1,256,256]{3,4,1,2,0:T(8,128)(2,1)S(1)}, bf16[8,4,1,256,256]{3,4,1,2,0:T(8,128)(2,1)S(1)}) fusion(bf16[8,4,1,256,256]{3,4,1,2,0:T(8,128)(2,1)} %copy.125, bf16[8,4,1,256,256]{3,4,1,2,0:T(8,128)(2,1)} %copy.126, pred[8,4]{1,0:T(8,128)(4,1)S(1)} %bitcast.198, pred[8,4]{1,0:T(8,128)(4,1)S(1)} %bitcast.207, ...), kind=kLoop, calls=%fused_computation.57 | loop fusion | flops 8388608 | bytes 16777344 | tf_op jit(solution)/shard_map/jit(_where)/select_n | solution.py:23
  82.7 6.5 %fusion = f32[8,2,256,256,1]{3,2,4,1,0:T(8,128)} fusion(bf16[8,4,1,256,256]{3,4,1,2,0:T(8,128)(2,1)S(1)} %get-tuple-element.81, bf16[8,4,1,256,256]{3,4,1,2,0:T(8,128)(2,1)S(1)} %get-tuple-element.80, bf16[8,6,256,256]{3,2,1,0:T(8,128)(2,1)} %param.9), kind=kOutput, calls=%fused_computation.10 | convolution fusion | flops 2151677952 | bytes 16777216 | tf_op jit(solution)/shard_map/rkab,rknbc->rnac/dot_general | solution.py:30
  89.2 6.5 %fusion.30 = bf16[8,2,256,256]{2,3,1,0:T(8,128)(2,1)S(1)} fusion(bf16[8,2,256,256]{2,3,1,0:T(8,128)(2,1)} %copy.63, f32[8,2,256,256,1]{3,2,4,1,0:T(8,128)} %fusion, bf16[8,2,1,256,256]{3,4,1,2,0:T(8,128)(2,1)} %get-tuple-element.89, bf16[8,2,1,256,256]{3,4,1,2,0:T(8,128)(2,1)} %get-tuple-element.88, bf16[8,6,256,256]{3,2,1,0:T(8,128)(2,1)} %param.9, ...), kind=kOutput, calls=%fused_computation.48 | convolution fusion | flops 1617952768 | bytes 15728640 | tf_op jit(solution)/shard_map/rab,rnbc->rnac/dot_general | solution.py:82
  95.7 2.1 gather_fusion.4
  97.8 4.3 %all-to-all-start.1 = ((bf16[8,2,256,256]{2,3,1,0:T(8,128)(2,1)}), bf16[8,2,256,256]{2,3,1,0:T(8,128)(2,1)}, u32[]{:S(2)}, u32[]{:S(2)}) async-start(bf16[8,2,256,256]{2,3,1,0:T(8,128)(2,1)} %gather_fusion.4), calls=%async_computation.1 | async-start | bytes 4194304 | tf_op jit(solution)/shard_map/all_to_all | solution.py:35
  102.2 2.8 gather_fusion.3
  105.0 4.5 %collective-permute-start.2 = (bf16[1,2,256,256]{2,3,1,0:T(8,128)(2,1)S(1)}, bf16[1,2,256,256]{2,3,1,0:T(8,128)(2,1)S(1)}, u32[]{:S(2)}, u32[]{:S(2)}) collective-permute-start(bf16[1,2,256,256]{2,3,1,0:T(8,128)(2,1)S(1)} %get-tuple-element.94), channel_id=1, source_target_pairs={{0,8},{8,16},{16,24},{1,9},{9,17},{17,25},{2,10},{10,18},{18,26},{... | collective-permute-start | bytes 786440 | tf_op jit(solution)/shard_map/ppermute | solution.py:14
  109.5 1.5 collective-permute-start.3
  111.0 2.4 select_select_fusion.9
  113.4 4.9 %fusion.16 = f32[8,2,256,256,1]{3,2,4,1,0:T(8,128)} fusion(bf16[8,2,1,256,256]{3,4,1,2,0:T(8,128)(2,1)S(1)} %get-tuple-element.87, bf16[8,2,1,256,256]{3,4,1,2,0:T(8,128)(2,1)S(1)} %get-tuple-element.86, bf16[8,6,256,256]{3,2,1,0:T(8,128)(2,1)} %param.9), kind=kOutput, calls=%fused_computation.30 | convolution fusion | flops 1075838976 | bytes 10485760 | tf_op jit(solution)/shard_map/rkab,rknbc->rnac/dot_general | solution.py:30
  118.4 1.3 collective-permute-done.3
  119.7 9.1 %all-to-all-done.1 = bf16[8,2,256,256]{2,3,1,0:T(8,128)(2,1)} async-done(((bf16[8,2,256,256]{2,3,1,0:T(8,128)(2,1)}), bf16[8,2,256,256]{2,3,1,0:T(8,128)(2,1)}, u32[]{:S(2)}, u32[]{:S(2)}) %all-to-all-start.1) | async-done | bytes 2097184 | tf_op jit(solution)/shard_map/all_to_all | solution.py:35
  128.8 3.4 %pad_maximum_fusion.1 = bf16[10,2,256,256]{2,3,1,0:T(8,128)(2,1)} fusion(bf16[1,2,256,256]{2,3,1,0:T(8,128)(2,1)S(1)} %collective-permute-done.3, bf16[1,2,256,256]{2,3,1,0:T(8,128)(2,1)S(1)} %collective-permute-done.2, bf16[8,2,256,256]{2,3,1,0:T(8,128)(2,1)} %all-to-all-done.1), kind=kLoop, calls=%fused_computation.62 | loop fusion | flops 2621440 | bytes 5242880 | tf_op jit(solution)/shard_map/concatenate | solution.py:38
  132.2 6.8 %gather_fusion.5 = bf16[32,2,256,256]{2,3,1,0:T(8,128)(2,1)} fusion(bf16[10,2,256,256]{2,3,1,0:T(8,128)(2,1)} %pad_maximum_fusion.1, s32[1024]{0:T(1024)S(1)} %pad_clamp_fusion), kind=kCustom, calls=%fused_computation.5 | custom fusion | bytes 16777344 | tf_op jit(solution)/shard_map/gather | solution.py:29
  139.0 5.8 %select_select_fusion.3 = (bf16[8,4,1,256,256]{3,4,1,2,0:T(8,128)(2,1)}, bf16[8,4,1,256,256]{3,4,1,2,0:T(8,128)(2,1)}) fusion(pred[8,4]{1,0:T(8,128)(4,1)S(1)} %bitcast.199, pred[8,4]{1,0:T(8,128)(4,1)S(1)} %bitcast.208, bf16[8,4,2,256,256]{3,4,2,1,0:T(8,128)(2,1)} %bitcast.192, pred[8,4]{1,0:T(8,128)(4,1)S(1)} %bitcast.205, pred[8,4]{1,0:T(8,128)(4,1)S(1)} %bitcast.202), kind=kLoop, calls=%fused_computation.55 | loop fusion | flops 8388608 | bytes 16777344 | tf_op jit(solution)/shard_map/jit(_where)/select_n | solution.py:23
  144.8 8.0 %fusion.25 = bf16[8,2,256,256]{2,3,1,0:T(8,128)(2,1)S(1)} fusion(bf16[8,2,256,256]{2,3,1,0:T(8,128)(2,1)} %copy-done.5, f32[8,2,256,256,1]{3,2,4,1,0:T(8,128)} %fusion.16, bf16[8,4,1,256,256]{3,4,1,2,0:T(8,128)(2,1)} %get-tuple-element.79, bf16[8,4,1,256,256]{3,4,1,2,0:T(8,128)(2,1)} %get-tuple-element.78, bf16[8,6,256,256]{3,2,1,0:T(8,128)(2,1)} %param.9, ...), kind=kOutput, calls=%fused_computation.41 | convolution fusion | flops 2693791744 | bytes 22020096 | tf_op jit(solution)/shard_map/rab,rnbc->rnac/dot_general | solution.py:82
  152.8 2.1 gather_fusion.7
  154.9 4.3 %all-to-all-start.2 = ((bf16[8,2,256,256]{2,3,1,0:T(8,128)(2,1)}), bf16[8,2,256,256]{2,3,1,0:T(8,128)(2,1)}, u32[]{:S(2)}, u32[]{:S(2)}) async-start(bf16[8,2,256,256]{2,3,1,0:T(8,128)(2,1)} %gather_fusion.7), calls=%async_computation.2 | async-start | bytes 4194304 | tf_op jit(solution)/shard_map/all_to_all | solution.py:35
  159.2 0.1 copy.84
  159.4 2.8 gather_fusion.6
  162.2 4.5 %collective-permute-start.4 = (bf16[1,2,256,256]{2,3,1,0:T(8,128)(2,1)S(1)}, bf16[1,2,256,256]{2,3,1,0:T(8,128)(2,1)S(1)}, u32[]{:S(2)}, u32[]{:S(2)}) collective-permute-start(bf16[1,2,256,256]{2,3,1,0:T(8,128)(2,1)S(1)} %get-tuple-element.92), channel_id=1, source_target_pairs={{0,8},{8,16},{16,24},{1,9},{9,17},{17,25},{2,10},{10,18},{18,26},{... | collective-permute-start | bytes 786440 | tf_op jit(solution)/shard_map/ppermute | solution.py:14
  166.7 1.3 collective-permute-start.5
  168.0 2.4 select_select_fusion.7
  170.5 4.9 %fusion.20 = f32[8,2,256,256,1]{3,2,4,1,0:T(8,128)} fusion(bf16[8,2,1,256,256]{3,4,1,2,0:T(8,128)(2,1)S(1)} %get-tuple-element.85, bf16[8,2,1,256,256]{3,4,1,2,0:T(8,128)(2,1)S(1)} %get-tuple-element.84, bf16[8,6,256,256]{3,2,1,0:T(8,128)(2,1)} %param.9), kind=kOutput, calls=%fused_computation.34 | convolution fusion | flops 1075838976 | bytes 10485760 | tf_op jit(solution)/shard_map/rkab,rknbc->rnac/dot_general | solution.py:30
  175.4 1.5 collective-permute-done.5
  176.9 8.9 %all-to-all-done.2 = bf16[8,2,256,256]{2,3,1,0:T(8,128)(2,1)} async-done(((bf16[8,2,256,256]{2,3,1,0:T(8,128)(2,1)}), bf16[8,2,256,256]{2,3,1,0:T(8,128)(2,1)}, u32[]{:S(2)}, u32[]{:S(2)}) %all-to-all-start.2) | async-done | bytes 2097184 | tf_op jit(solution)/shard_map/all_to_all | solution.py:35
  185.8 1.9 pad_maximum_fusion.2
  187.8 5.1 %gather_fusion.8 = bf16[32,2,256,256]{2,3,1,0:T(8,128)(2,1)} fusion(bf16[10,2,256,256]{2,3,1,0:T(8,128)(2,1)S(1)} %pad_maximum_fusion.2, s32[1024]{0:T(1024)S(1)} %pad_clamp_fusion), kind=kCustom, calls=%fused_computation.8 | custom fusion | bytes 16777344 | tf_op jit(solution)/shard_map/gather | solution.py:29
  192.8 6.0 %select_select_fusion.1 = (bf16[8,4,1,256,256]{3,4,1,2,0:T(8,128)(2,1)}, bf16[8,4,1,256,256]{3,4,1,2,0:T(8,128)(2,1)}) fusion(pred[8,4]{1,0:T(8,128)(4,1)S(1)} %bitcast.200, pred[8,4]{1,0:T(8,128)(4,1)S(1)} %bitcast.209, bf16[8,4,2,256,256]{3,4,2,1,0:T(8,128)(2,1)} %bitcast.191, pred[8,4]{1,0:T(8,128)(4,1)S(1)} %bitcast.206, pred[8,4]{1,0:T(8,128)(4,1)S(1)} %bitcast.203), kind=kLoop, calls=%fused_computation.53 | loop fusion | flops 8388608 | bytes 16777344 | tf_op jit(solution)/shard_map/jit(_where)/select_n | solution.py:23
  198.8 9.0 %convert_bitcast_fusion = bf16[8,2,2,256,256]{3,4,1,2,0:T(8,128)(2,1)} fusion(f32[8,2,256,256,1]{3,2,4,1,0:T(8,128)} %fusion.20, bf16[8,4,1,256,256]{3,4,1,2,0:T(8,128)(2,1)} %get-tuple-element.77, bf16[8,4,1,256,256]{3,4,1,2,0:T(8,128)(2,1)} %get-tuple-element.76, bf16[8,6,256,256]{3,2,1,0:T(8,128)(2,1)} %param.9, bf16[8,2,256,256]{2,3,1,0:T(8,128)(2,1)S(1)} %copy-done.4), kind=kOutput, calls=%fused_computation.51 | convolution fusion | flops 3229614080 | bytes 23068672 | tf_op jit(solution)/shard_map/rnab,rmac->rnmbc/dot_general | solution.py:89
  207.8 6.5 %copy.92 = bf16[8,2,2,256,256]{4,3,2,1,0:T(8,128)(2,1)} copy(bf16[8,2,2,256,256]{3,4,1,2,0:T(8,128)(2,1)} %convert_bitcast_fusion) | data formatting | bytes 8388608 | tf_op jit(solution)/shard_map/convert_element_type | solution.py:92
  214.3 3.4 %broadcast_in_dim.157 = bf16[48,256,256]{2,1,0:T(8,128)(2,1)} broadcast(bf16[]{:T(256)} %constant.12.clone.1), dimensions={} | broadcast | bytes 6291458 | tf_op jit(solution)/shard_map/broadcast_in_dim | solution.py:94
  217.7 11.3 %scatter_fusion = bf16[48,256,256]{2,1,0:T(8,128)(2,1)} fusion(bf16[48,256,256]{2,1,0:T(8,128)(2,1)} %broadcast_in_dim.157, s32[32]{0:T(128)S(1)} %fusion.76, bf16[32,256,256]{2,1,0:T(8,128)(2,1)} %bitcast.194), kind=kCustom, calls=%fused_computation.9 | custom fusion | bytes 12583040 | tf_op jit(solution)/shard_map/scatter | solution.py:96
  229.0 4.7 %all-to-all-start.3 = ((bf16[48,256,256]{2,1,0:T(8,128)(2,1)}), bf16[48,256,256]{2,1,0:T(8,128)(2,1)}, u32[]{:S(2)}, u32[]{:S(2)}) async-start(bf16[48,256,256]{2,1,0:T(8,128)(2,1)} %scatter_fusion), calls=%async_computation.3 | async-start | bytes 12582912 | tf_op jit(solution)/shard_map/all_to_all | solution.py:98
  233.7 2.4 copy.93
  236.1 69.2 %all-to-all-done.3 = bf16[48,256,256]{2,1,0:T(8,128)(2,1)} async-done(((bf16[48,256,256]{2,1,0:T(8,128)(2,1)}), bf16[48,256,256]{2,1,0:T(8,128)(2,1)}, u32[]{:S(2)}, u32[]{:S(2)}) %all-to-all-start.3) | async-done | bytes 6291488 | tf_op jit(solution)/shard_map/all_to_all | solution.py:98
  305.3 4.8 %reduce_sum.12 = bf16[6,256,256]{2,1,0:T(8,128)(2,1)} reduce(bf16[8,6,256,256]{3,2,1,0:T(8,128)(2,1)} %bitcast.60, bf16[]{:T(256)} %constant.12.clone.1), dimensions={0}, to_apply=%region_1.2 | reduce | flops 2752512 | bytes 7077890 | tf_op jit(solution)/shard_map/reduce_sum | solution.py:99
  (39 shorter events, 0.6 us)
Async XLA Ops:
  0.6 88.6 %copy-start = (bf16[8,256,256]{2,1,0:T(8,128)(2,1)S(1)}, bf16[8,256,256]{2,1,0:T(8,128)(2,1)}, u32[]{:S(2)}) copy-start(bf16[8,256,256]{2,1,0:T(8,128)(2,1)} %param.14) | copy-start | bytes 3145732
  7.7 37.0 %collective-permute-start = (bf16[1,2,256,256]{3,2,1,0:T(8,128)(2,1)}, bf16[1,2,256,256]{3,2,1,0:T(8,128)(2,1)S(1)}, u32[]{:S(2)}, u32[]{:S(2)}) collective-permute-start(bf16[1,2,256,256]{3,2,1,0:T(8,128)(2,1)} %get-tuple-element.96), channel_id=1, source_target_pairs={{0,8},{8,16},{16,24},{1,9},{9,17},{17,25},{2,10},{10,18},{18,26},{... | collective-permute-start | bytes 786440 | tf_op jit(solution)/shard_map/ppermute | solution.py:14
  12.7 32.0 %collective-permute-start.1 = (bf16[1,2,256,256]{3,2,1,0:T(8,128)(2,1)}, bf16[1,2,256,256]{3,2,1,0:T(8,128)(2,1)}, u32[]{:S(2)}, u32[]{:S(2)}) collective-permute-start(bf16[1,2,256,256]{3,2,1,0:T(8,128)(2,1)} %get-tuple-element.97), channel_id=1, source_target_pairs={{8,0},{16,8},{24,16},{9,1},{17,9},{25,17},{10,2},{18,10},{26,18},{... | collective-permute-start | bytes 786440 | tf_op jit(solution)/shard_map/ppermute | solution.py:14
  14.7 8.3 %copy-start.8 = (s32[8,4]{0,1:T(4,128)S(1)}, s32[8,4]{0,1:T(4,128)}, u32[]{:S(2)}) copy-start(s32[8,4]{0,1:T(4,128)} %param.11) | copy-start | bytes 388
  14.7 8.3 %copy-start.2 = (bf16[8,2,256,256]{3,2,1,0:T(8,128)(2,1)S(1)}, bf16[8,2,256,256]{3,2,1,0:T(8,128)(2,1)}, u32[]{:S(2)}) copy-start(bf16[8,2,256,256]{3,2,1,0:T(8,128)(2,1)} %param.13) | copy-start | bytes 6291460
  18.5 7.1 %copy-start.6 = (s32[8,6,2]{0,2,1:T(2,128)S(1)}, s32[8,6,2]{0,2,1:T(2,128)}, u32[]{:S(2)}) copy-start(s32[8,6,2]{0,2,1:T(2,128)} %param.12) | copy-start | bytes 1156
  18.5 7.5 %copy-start.9 = (s32[8,2]{0,1:T(2,128)S(1)}, s32[8,2]{0,1:T(2,128)}, u32[]{:S(2)}) copy-start(s32[8,2]{0,1:T(2,128)} %param.10) | copy-start | bytes 196
  18.5 31.1 %all-to-all-start = ((bf16[8,2,256,256]{3,2,1,0:T(8,128)(2,1)}), bf16[8,2,256,256]{3,2,1,0:T(8,128)(2,1)}, u32[]{:S(2)}, u32[]{:S(2)}) async-start(bf16[8,2,256,256]{3,2,1,0:T(8,128)(2,1)} %gather_fusion.1), calls=%async_computation | async-start | bytes 4194304 | tf_op jit(solution)/shard_map/all_to_all | solution.py:35
  95.7 9.2 %copy-start.5 = (bf16[8,2,256,256]{2,3,1,0:T(8,128)(2,1)}, bf16[8,2,256,256]{2,3,1,0:T(8,128)(2,1)S(1)}, u32[]{:S(2)}) copy-start(bf16[8,2,256,256]{2,3,1,0:T(8,128)(2,1)S(1)} %fusion.30) | copy-start | bytes 6291460
  97.8 31.0 %all-to-all-start.1 = ((bf16[8,2,256,256]{2,3,1,0:T(8,128)(2,1)}), bf16[8,2,256,256]{2,3,1,0:T(8,128)(2,1)}, u32[]{:S(2)}, u32[]{:S(2)}) async-start(bf16[8,2,256,256]{2,3,1,0:T(8,128)(2,1)} %gather_fusion.4), calls=%async_computation.1 | async-start | bytes 4194304 | tf_op jit(solution)/shard_map/all_to_all | solution.py:35
  105.0 13.4 %collective-permute-start.2 = (bf16[1,2,256,256]{2,3,1,0:T(8,128)(2,1)S(1)}, bf16[1,2,256,256]{2,3,1,0:T(8,128)(2,1)S(1)}, u32[]{:S(2)}, u32[]{:S(2)}) collective-permute-start(bf16[1,2,256,256]{2,3,1,0:T(8,128)(2,1)S(1)} %get-tuple-element.94), channel_id=1, source_target_pairs={{0,8},{8,16},{16,24},{1,9},{9,17},{17,25},{2,10},{10,18},{18,26},{... | collective-permute-start | bytes 786440 | tf_op jit(solution)/shard_map/ppermute | solution.py:14
  109.5 10.2 %collective-permute-start.3 = (bf16[1,2,256,256]{2,3,1,0:T(8,128)(2,1)S(1)}, bf16[1,2,256,256]{2,3,1,0:T(8,128)(2,1)S(1)}, u32[]{:S(2)}, u32[]{:S(2)}) collective-permute-start(bf16[1,2,256,256]{2,3,1,0:T(8,128)(2,1)S(1)} %get-tuple-element.95), channel_id=1, source_target_pairs={{8,0},{16,8},{24,16},{9,1},{17,9},{25,17},{10,2},{18,10},{26,18},{... | collective-permute-start | bytes 786440 | tf_op jit(solution)/shard_map/ppermute | solution.py:14
  152.8 9.4 %copy-start.3 = (bf16[8,2,256,256]{2,3,1,0:T(8,128)(2,1)}, bf16[8,2,256,256]{2,3,1,0:T(8,128)(2,1)S(1)}, u32[]{:S(2)}) copy-start(bf16[8,2,256,256]{2,3,1,0:T(8,128)(2,1)S(1)} %fusion.25) | copy-start | bytes 6291460
  152.8 6.4 %copy-start.7 = (s32[8,2,2]{0,2,1:T(2,128)S(1)}, s32[8,2,2]{0,2,1:T(2,128)}, u32[]{:S(2)}) copy-start(s32[8,2,2]{0,2,1:T(2,128)} %param.17) | copy-start | bytes 388
  154.9 31.0 %all-to-all-start.2 = ((bf16[8,2,256,256]{2,3,1,0:T(8,128)(2,1)}), bf16[8,2,256,256]{2,3,1,0:T(8,128)(2,1)}, u32[]{:S(2)}, u32[]{:S(2)}) async-start(bf16[8,2,256,256]{2,3,1,0:T(8,128)(2,1)} %gather_fusion.7), calls=%async_computation.2 | async-start | bytes 4194304 | tf_op jit(solution)/shard_map/all_to_all | solution.py:35
  162.2 13.2 %collective-permute-start.4 = (bf16[1,2,256,256]{2,3,1,0:T(8,128)(2,1)S(1)}, bf16[1,2,256,256]{2,3,1,0:T(8,128)(2,1)S(1)}, u32[]{:S(2)}, u32[]{:S(2)}) collective-permute-start(bf16[1,2,256,256]{2,3,1,0:T(8,128)(2,1)S(1)} %get-tuple-element.92), channel_id=1, source_target_pairs={{0,8},{8,16},{16,24},{1,9},{9,17},{17,25},{2,10},{10,18},{18,26},{... | collective-permute-start | bytes 786440 | tf_op jit(solution)/shard_map/ppermute | solution.py:14
  166.7 10.2 %collective-permute-start.5 = (bf16[1,2,256,256]{2,3,1,0:T(8,128)(2,1)S(1)}, bf16[1,2,256,256]{2,3,1,0:T(8,128)(2,1)S(1)}, u32[]{:S(2)}, u32[]{:S(2)}) collective-permute-start(bf16[1,2,256,256]{2,3,1,0:T(8,128)(2,1)S(1)} %get-tuple-element.93), channel_id=1, source_target_pairs={{8,0},{16,8},{24,16},{9,1},{17,9},{25,17},{10,2},{18,10},{26,18},{... | collective-permute-start | bytes 786440 | tf_op jit(solution)/shard_map/ppermute | solution.py:14
  192.8 6.0 %copy-start.4 = (bf16[8,2,256,256]{2,3,1,0:T(8,128)(2,1)S(1)}, bf16[8,2,256,256]{2,3,1,0:T(8,128)(2,1)}, u32[]{:S(2)}) copy-start(bf16[8,2,256,256]{2,3,1,0:T(8,128)(2,1)} %copy-done.3) | copy-start | bytes 6291460
  229.0 76.3 %all-to-all-start.3 = ((bf16[48,256,256]{2,1,0:T(8,128)(2,1)}), bf16[48,256,256]{2,1,0:T(8,128)(2,1)}, u32[]{:S(2)}, u32[]{:S(2)}) async-start(bf16[48,256,256]{2,1,0:T(8,128)(2,1)} %scatter_fusion), calls=%async_computation.3 | async-start | bytes 12582912 | tf_op jit(solution)/shard_map/all_to_all | solution.py:98
  233.7 76.4 %copy-start.1 = (bf16[8,256,256]{2,1,0:T(8,128)(2,1)S(1)}, bf16[8,256,256]{2,1,0:T(8,128)(2,1)}, u32[]{:S(2)}) copy-start(bf16[8,256,256]{2,1,0:T(8,128)(2,1)} %param.14) | copy-start | bytes 3145732
where the time goes:
time: 312 us; the launch traced here: 310 us
  local copies, waits for them, and re-layouts  95.7 us (31%)
  waiting for transfers between devices  94.9 us (30%)
  matrix products  39.8 us (13%)
  other arithmetic  38.9 us (12%)
  starting transfers between devices  35.9 us (12%)
  between operations  4.8 us (2%)
    all_to_all x1, waiting for transfers between devices, body(): lax.all_to_all(slot_blocks, 'gy', split_axis=0, concat_axis=0, tiled=True)  69.2 us
    gather x6, local copies, waits for them, and re-layouts, block_product(): chosen = select_blocks(lookup[columns], matches)  27 us
    unnamed x27, local copies, waits for them, and re-layouts  24.6 us
    select_n x6, other arithmetic, select_blocks(): chosen = jnp.where(matched, picked[:, :, in_block], chosen)  24.5 us
    all_to_all x3, waiting for transfers between devices, fetch_remote(): lax.all_to_all(outgoing, 'gy', split_axis=0, concat_axis=0, tiled=True)  22.9 us
    ppermute x6, starting transfers between devices, from_behind(): lax.ppermute(value, axis, [(source, source + steps) for source in range(l...  18 us
    dot_general x3, matrix products, block_product(): jnp.einsum('rkab,rknbc->rnac', blocks, chosen, preferred_element_type=jnp...  16.3 us
    dot_general x2, matrix products, body(): jnp.einsum('rab,rnbc->rnac', inverse_diagonal, image, preferred_element_t...  14.5 us
  transfers between devices with their start and end apart: 10, of which 6 were waited for; matrix products, arithmetic and copies ran while one was open for 16% of the time, Pallas kernels for 0%

commit v1 on v0

v1 whole, which is shorter than its diff:
```python
import functools

import jax
import jax.numpy as jnp
from jax import lax
from jax.experimental import pallas as pl
from jax.experimental.pallas import tpu as pltpu
from jax.sharding import PartitionSpec as P

MESH = pl.DeviceIdType.MESH


def gather_order(me, group, owned):
    bits = group.bit_length() - 1
    place = jnp.arange(group, dtype=jnp.int32)
    high = place // (group // 2)
    odd = (high + me) % 2
    other = high
    for step in range(1, bits):
        bit = (place >> (bits - 1 - step)) & 1
        other = other | jnp.where(odd == 0, bit << step, bit << (bits - step))
    owner = me ^ other
    slots = owner[:, None] * owned + jnp.arange(owned, dtype=jnp.int32)[None, :]
    return slots.reshape(-1)


def kernel(
    dims,
    local_ref,
    remote_ref,
    match_ref,
    peer_ref,
    slab_ref,
    inverse_ref,
    operator_hbm,
    tentative_hbm,
    diagonal_hbm,
    smooth_hbm,
    coarse_ref,
    operator,
    diagonal,
    own_a,
    own_b,
    rem_a,
    rem_b,
    send,
    local_sum,
    partial,
    half_send,
    total,
    *rest,
):
    slabs, group, rows, kl, ko, kp, peers, halo, owned = dims
    bits = group.bit_length() - 1
    landed = rest[:bits]
    load_sem, out_sem, send_sem, recv_sem, slab_send_sem, slab_recv_sem, half_send_sem, half_recv_sem = rest[bits:]
    width = operator.shape[-1]
    gx = lax.axis_index("gx")
    me = lax.axis_index("gy")
    has_below = gx > 0
    has_above = gx < slabs - 1
    own_zero = rows * kp
    rem_zero = (group * peers + 2 * halo) * kp
    span = peers * kp
    slab_span = halo * kp
    slab_at = group * span
    send_slab_at = group * span

    load_rows = pltpu.make_async_copy(tentative_hbm, own_a.at[pl.ds(0, own_zero)], load_sem.at[0])
    load_rows.start()
    load_operator = pltpu.make_async_copy(operator_hbm, operator, load_sem.at[1])
    load_operator.start()
    load_diagonal = pltpu.make_async_copy(diagonal_hbm, diagonal, load_sem.at[2])
    load_diagonal.start()

    barrier = pltpu.get_barrier_semaphore()

    def greet(offset, carry):
        pl.semaphore_signal(
            barrier, inc=1, device_id=(gx, (me + offset) % group), device_id_type=MESH
        )
        return carry

    lax.fori_loop(1, group, greet, 0)

    @pl.when(has_below)
    def _():
        pl.semaphore_signal(barrier, inc=1, device_id=(gx - 1, me), device_id_type=MESH)

    @pl.when(has_above)
    def _():
        pl.semaphore_signal(barrier, inc=1, device_id=(gx + 1, me), device_id_type=MESH)

    zero = jnp.zeros((width, width), jnp.bfloat16)
    own_a[own_zero] = zero
    own_b[own_zero] = zero
    rem_a[rem_zero] = zero
    rem_b[rem_zero] = zero
    partial[rows * kp * kp] = zero
    neighbours = jnp.where(has_below, 1, 0) + jnp.where(has_above, 1, 0)
    pl.semaphore_wait(barrier, group - 1 + neighbours)

    load_rows.wait()

    def stage(own, row, buffer, at):
        for n in range(kp):
            buffer[at + n] = own[row * kp + n]

    def peer_copy(step, rem, offset):
        target = (me + offset) % group
        return pltpu.make_async_remote_copy(
            src_ref=send.at[pl.ds(offset * span, span)],
            dst_ref=rem.at[pl.ds(me * span, span)],
            send_sem=send_sem.at[step, offset],
            recv_sem=recv_sem.at[step, offset],
            device_id=(gx, target),
            device_id_type=MESH,
        )

    def slab_copy(step, rem, way):
        return pltpu.make_async_remote_copy(
            src_ref=send.at[pl.ds(send_slab_at + way * slab_span, slab_span)],
            dst_ref=rem.at[pl.ds(slab_at + way * slab_span, slab_span)],
            send_sem=slab_send_sem.at[step, way],
            recv_sem=slab_recv_sem.at[step, way],
            device_id=(gx + 1 - 2 * way, me),
            device_id_type=MESH,
        )

    for step in range(3):
        own, after = (own_a, own_b) if step % 2 == 0 else (own_b, own_a)
        rem = rem_a if step % 2 == 0 else rem_b

        def post(offset, carry):
            target = (me + offset) % group
            for s in range(peers):
                stage(own, peer_ref[0, target * peers + s], send, offset * span + s * kp)
            peer_copy(step, rem, offset).start()
            return carry

        lax.fori_loop(1, group, post, 0)
        for way, present in enumerate((has_above, has_below)):

            @pl.when(present)
            def _():
                for h in range(halo):
                    stage(
                        own,
                        slab_ref[0, way * halo + h],
                        send,
                        send_slab_at + way * slab_span + h * kp,
                    )
                slab_copy(step, rem, way).start()

        for s in range(peers):
            stage(own, peer_ref[0, me * peers + s], rem, me * span + s * kp)

        if step == 0:
            load_operator.wait()
        if step == 2:
            store_rows = pltpu.make_async_copy(own.at[pl.ds(0, own_zero)], smooth_hbm, out_sem)
            store_rows.start()

        def local_row(row, carry):
            for n in range(kp):
                value = None
                for k in range(kl):
                    match = match_ref[row, k * kp + n]
                    at = jnp.where(match == kp, own_zero, local_ref[row, k] * kp + match)
                    term = jnp.dot(operator[row, k], own[at], preferred_element_type=jnp.float32)
                    value = term if value is None else value + term
                local_sum[row * kp + n] = value
            return carry

        lax.fori_loop(0, rows, local_row, 0)
        if step == 0:
            load_diagonal.wait()

        def finish(offset, carry):
            peer_copy(step, rem, offset).wait()
            return carry

        lax.fori_loop(1, group, finish, 0)
        for way, (sends, receives) in enumerate(((has_above, has_below), (has_below, has_above))):

            @pl.when(sends)
            def _():
                slab_copy(step, rem, way).wait_send()

            @pl.when(receives)
            def _():
                slab_copy(step, rem, way).wait_recv()

        def remote_row(row, carry):
            images = []
            for n in range(kp):
                value = local_sum[row * kp + n]
                for k in range(ko):
                    match = match_ref[row, (kl + k) * kp + n]
                    source = jnp.maximum(remote_ref[row, k] - rows, 0)
                    from_below = (source >= group * peers) & (source < group * peers + halo)
                    from_above = source >= group * peers + halo
                    absent = (match == kp) | (from_below & (gx == 0)) | (from_above & (gx == slabs - 1))
                    at = jnp.where(absent, rem_zero, source * kp + match)
                    value += jnp.dot(
                        operator[row, kl + k], rem[at], preferred_element_type=jnp.float32
                    )
                images.append(value.astype(jnp.bfloat16))
            if step < 2:
                for n in range(kp):
                    update = jnp.dot(diagonal[row], images[n], preferred_element_type=jnp.float32)
                    before = own[row * kp + n].astype(jnp.float32)
                    after[row * kp + n] = (before - update).astype(jnp.bfloat16)
            else:
                for n1 in range(kp):
                    left = own[row * kp + n1]
                    for n2 in range(kp):
                        block = lax.dot_general(
                            left,
                            images[n2],
                            (((0,), (0,)), ((), ())),
                            preferred_element_type=jnp.float32,
                        )
                        partial[(row * kp + n1) * kp + n2] = block.astype(jnp.bfloat16)
            return carry

        lax.fori_loop(0, rows, remote_row, 0)

    core = me % 2

    def partner(step):
        def flip(bit):
            return me + bit * (1 - 2 * ((me // bit) % 2))

        if step == 0:
            return flip(1)
        return (1 - core) * flip(1 << step) + core * flip(1 << (bits - step))

    def pieces(length):
        middle = length // 2
        return ((middle, length - middle), (0, middle))

    def half_copy(step, piece, length):
        at, count = pieces(length)[piece]
        source = half_send.at[pl.ds(at, count)] if step == 0 else total.at[pl.ds(length + at, count)]
        return pltpu.make_async_remote_copy(
            src_ref=source,
            dst_ref=landed[step].at[pl.ds(at, count)],
            send_sem=half_send_sem.at[step, piece],
            recv_sem=half_recv_sem.at[step, piece],
            device_id=(gx, partner(step)),
            device_id_type=MESH,
        )

    length = group * owned // 2
    for piece in range(2):
        at, count = pieces(length)[piece]

        def pick(j, carry):
            half_send[at + j] = partial[inverse_ref[length + at + j]]
            return carry

        lax.fori_loop(0, count, pick, 0)
        half_copy(0, piece, length).start()

    for step in range(bits):
        last = step == bits - 1
        for piece in range(2):
            at, count = pieces(length)[piece]
            half_copy(step, piece, length).wait_recv()

            def add(j, carry):
                if step == 0:
                    mine = partial[inverse_ref[at + j]]
                else:
                    mine = total[at + j]
                value = mine.astype(jnp.float32) + landed[step][at + j].astype(jnp.float32)
                if last:
                    coarse_ref[at + j] = value.astype(jnp.bfloat16)
                else:
                    total[at + j] = value.astype(jnp.bfloat16)
                return carry

            lax.fori_loop(0, count, add, 0)
            if piece == 0 and not last:
                for sub in range(2):
                    half_copy(step + 1, sub, length // 2).start()
        length //= 2
    length = group * owned // 2
    for step in range(bits):
        for piece in range(2):
            half_copy(step, piece, length).wait_send()
        length //= 2
    store_rows.wait()


def body(
    operator_blocks,
    local_columns,
    remote_columns,
    match_slots,
    tentative,
    inverse_diagonal,
    peer_sends,
    slab_sends,
    coarse_slots,
):
    slabs = lax.axis_size("gx")
    group = lax.axis_size("gy")
    rows, kp, width = tentative.shape[:3]
    kl, ko = local_columns.shape[1], remote_columns.shape[1]
    peers = peer_sends.shape[1] // group
    halo = slab_sends.shape[1] // 2
    owned = (3 * rows * kp * kp // 2 + group - 1) // group
    bits = group.bit_length() - 1
    count = rows * kp * kp
    dims = (slabs, group, rows, kl, ko, kp, peers, halo, owned)

    slots = gather_order(lax.axis_index("gy"), group, owned)
    named = coarse_slots.reshape(-1)
    which = jnp.arange(count, dtype=jnp.int32) - count
    inverse = count + jnp.sum(
        jnp.where(slots[:, None] == named[None, :], which[None, :], 0), axis=1, dtype=jnp.int32
    )

    def blocks(n, dtype=jnp.bfloat16):
        return pltpu.VMEM((n, width, width), dtype)

    smem = pl.BlockSpec(memory_space=pltpu.SMEM)
    anywhere = pl.BlockSpec(memory_space=pl.ANY)
    half = group * owned // 2
    remote_count = (group * peers + 2 * halo) * kp
    smoothed, coarse = pl.pallas_call(
        functools.partial(kernel, dims),
        out_shape=(
            jax.ShapeDtypeStruct((rows * kp, width, width), jnp.bfloat16),
            jax.ShapeDtypeStruct((owned, width, width), jnp.bfloat16),
        ),
        in_specs=[smem] * 6 + [anywhere] * 3,
        out_specs=(anywhere, pl.BlockSpec(memory_space=pltpu.VMEM)),
        scratch_shapes=[
            pltpu.VMEM(operator_blocks.shape, jnp.bfloat16),
            blocks(rows),
            blocks(rows * kp + 1),
            blocks(rows * kp + 1),
            blocks(remote_count + 1),
            blocks(remote_count + 1),
            blocks(remote_count),
            blocks(rows * kp, jnp.float32),
            blocks(count + 1),
            blocks(half),
            blocks(half),
            *[blocks(half >> step) for step in range(bits)],
            pltpu.SemaphoreType.DMA((3,)),
            pltpu.SemaphoreType.DMA,
            pltpu.SemaphoreType.DMA((3, group)),
            pltpu.SemaphoreType.DMA((3, group)),
            pltpu.SemaphoreType.DMA((3, 2)),
            pltpu.SemaphoreType.DMA((3, 2)),
            pltpu.SemaphoreType.DMA((bits, 2)),
            pltpu.SemaphoreType.DMA((bits, 2)),
        ],
        compiler_params=pltpu.CompilerParams(
            collective_id=0, has_side_effects=True, vmem_limit_bytes=67_000_000
        ),
    )(
        local_columns,
        remote_columns,
        match_slots.reshape(rows, -1),
        peer_sends,
        slab_sends,
        inverse,
        operator_blocks,
        tentative.reshape(rows * kp, width, width),
        inverse_diagonal,
    )
    return smoothed.reshape(tentative.shape), coarse


def solution(mesh):
    placed = (
        P(("gx", "gy"), None, None, None),
        P(("gx", "gy"), None),
        P(("gx", "gy"), None),
        P(("gx", "gy"), None, None),
        P(("gx", "gy"), None, None, None),
        P(("gx", "gy"), None, None),
        P(("gx", "gy"), None),
        P(("gx", "gy"), None),
        P(("gx", "gy"), None, None),
    )
    return jax.shard_map(
        body,
        mesh=mesh,
        in_specs=placed,
        out_specs=(P(("gx", "gy"), None, None, None), P(("gx", "gy"), None, None)),
        check_vma=False,
    )
```

time: 312 us -> 136 us (0.44)
  Pallas kernels: 0 us -> 125 us
  waiting for transfers between devices: 94.9 us -> 0 us
  local copies, waits for them, and re-layouts: 95.7 us -> 9.06 us
  matrix products: 39.8 us -> 0 us
  other arithmetic: 38.9 us -> 0.7 us
  starting transfers between devices: 35.9 us -> 0 us
  between operations: 4.8 us -> 0.67 us
    pallas_call x0 -> x1, Pallas kernels: none -> 125 us  [body(): pl.pallas_call(functools.partial(kernel, dims), out_shape=(jax.ShapeDtype...]
    all_to_all x4 -> x0, waiting for transfers between devices: 92.1 us -> none  [the longest x1 69.2 us: body(): lax.all_to_all(slot_blocks, 'gy', split_axis=0, concat_axis=0, tiled=True)]
    dot_general x6 -> x0, matrix products: 39.8 us -> none  [the longest x3 16.3 us: block_product(): jnp.einsum('rkab,rknbc->rnac', blocks, chosen, preferred_element_type=jnp...]
    gather x12 -> x0, local copies, waits for them, and re-layouts: 36.9 us -> none  [the longest x6 27 us: block_product(): chosen = select_blocks(lookup[columns], matches)]
    select_n x10 -> x0, other arithmetic: 25.2 us -> none  [the longest x6 24.5 us: select_blocks(): chosen = jnp.where(matched, picked[:, :, in_block], chosen)]
    ppermute x6 -> x0, starting transfers between devices: 18 us -> none  [from_behind(): lax.ppermute(value, axis, [(source, source + steps) for source in range(l...]
    all_to_all x4 -> x0, starting transfers between devices: 17.9 us -> none  [the longest x3 13.2 us: fetch_remote(): lax.all_to_all(outgoing, 'gy', split_axis=0, concat_axis=0, tiled=True)]
    unnamed x27 -> x7, local copies, waits for them, and re-layouts: 24.6 us -> 7.51 us
  transfers between devices with their start and end apart: 10 -> 0, of which waited for: 6 -> 0; matrix products, arithmetic and copies ran while one was open for 16% -> 0% of each run, Pallas kernels for 0% -> 0%
where the time goes in v1:
time: 136 us
  Pallas kernels  125 us (92%)
  local copies, waits for them, and re-layouts  9.06 us (7%)
    pallas_call x1, Pallas kernels, body(): pl.pallas_call(functools.partial(kernel, dims), out_shape=(jax.ShapeDtype...  125 us
    unnamed x7, local copies, waits for them, and re-layouts  7.51 us

profile of v1, /device:TPU:0, one launch (start us, length us, event | category | flops | bytes accessed | tf_op | source)
XLA Modules:
  0.0 135.7 jit_solution(7639415395609350774)
XLA Ops:
  0.7 0.1 iota_add_fusion
  0.7 0.1 add.59
  0.8 1.3 copy.20.local_ref
  2.2 1.3 copy.21.remote_ref
  3.5 0.7 reshape.75
  4.2 0.7 copy.22.match_ref
  4.9 0.8 copy.19
  5.6 0.1 eq.27
  5.7 0.1 select_reduce_fusion
  5.8 0.5 broadcast_add_fusion.inverse_ref
  6.4 125.3 %shard_map.104 = (bf16[16,256,256]{2,1,0:T(8,128)(2,1)}, bf16[6,256,256]{2,1,0:T(8,128)(2,1)}) custom-call(s32[8,2]{1,0:T(8,128)} %copy.20.local_ref, s32[8,4]{1,0:T(8,128)} %copy.21.remote_ref, s32[8,12]{1,0:T(8,128)} %copy.22.match_ref, s32[1,8]{1,0:T(1,128)} %peer_ref.1, s32[1,2]{1,0:T(1,128)} %slab_ref.1, s32[48]{0:T(128)} %broadcast_add_fusion.inverse_ref, ...), custom_call_target="tpu_custom_call" | custom-call | tf_op jit(solution)/shard_map/pallas_call | solution.py:333
  131.7 0.0 copy-start
  131.7 3.2 %copy.25 = bf16[8,2,256,256]{3,2,1,0:T(8,128)(2,1)} copy(bf16[8,2,256,256]{3,2,1,0:T(8,128)(2,1)} %bitcast.4) | data formatting | bytes 4194304
  134.8 0.0 copy-done
  134.9 0.9 copy.26
  (2 shorter events, 0.0 us)
Async XLA Ops:
  131.7 3.2 %copy-start = (bf16[6,256,256]{2,1,0:T(8,128)(2,1)S(1)}, bf16[6,256,256]{2,1,0:T(8,128)(2,1)}, u32[]{:S(2)}) copy-start(bf16[6,256,256]{2,1,0:T(8,128)(2,1)} %get-tuple-element.9) | copy-start | bytes 2359300

commit v2 on v1

--- a/solution.py
+++ b/solution.py
@@ -10,18 +10,17 @@
 MESH = pl.DeviceIdType.MESH
 
 
-def gather_order(me, group, owned):
+def gather_order(me, group, owned, shape):
     bits = group.bit_length() - 1
-    place = jnp.arange(group, dtype=jnp.int32)
+    at = lax.broadcasted_iota(jnp.int32, (group * owned, *shape), 0)
+    place = at // owned
     high = place // (group // 2)
     odd = (high + me) % 2
     other = high
     for step in range(1, bits):
         bit = (place >> (bits - 1 - step)) & 1
         other = other | jnp.where(odd == 0, bit << step, bit << (bits - step))
-    owner = me ^ other
-    slots = owner[:, None] * owned + jnp.arange(owned, dtype=jnp.int32)[None, :]
-    return slots.reshape(-1)
+    return (me ^ other) * owned + at % owned
 
 
 def kernel(
@@ -43,11 +42,10 @@
     own_b,
     rem_a,
     rem_b,
+    rem_c,
     send,
     local_sum,
     partial,
-    half_send,
-    total,
     *rest,
 ):
     slabs, group, rows, kl, ko, kp, peers, halo, owned = dims
@@ -96,6 +94,7 @@
     own_b[own_zero] = zero
     rem_a[rem_zero] = zero
     rem_b[rem_zero] = zero
+    rem_c[rem_zero] = zero
     partial[rows * kp * kp] = zero
     neighbours = jnp.where(has_below, 1, 0) + jnp.where(has_above, 1, 0)
     pl.semaphore_wait(barrier, group - 1 + neighbours)
@@ -127,33 +126,39 @@
             device_id_type=MESH,
         )
 
-    for step in range(3):
-        own, after = (own_a, own_b) if step % 2 == 0 else (own_b, own_a)
-        rem = rem_a if step % 2 == 0 else rem_b
-
-        def post(offset, carry):
+    rems = (rem_a, rem_b, rem_c)
+
+    def post_rows(step, rows_of):
+        rem = rems[step]
+
+        def post(turn, carry):
+            offset = 1 + (2 * turn + 1) % (group - 1)
             target = (me + offset) % group
-            for s in range(peers):
-                stage(own, peer_ref[0, target * peers + s], send, offset * span + s * kp)
+            for p in range(peers):
+                values = rows_of(peer_ref[0, target * peers + p])
+                for n in range(kp):
+                    send[offset * span + p * kp + n] = values[n]
             peer_copy(step, rem, offset).start()
             return carry
 
-        lax.fori_loop(1, group, post, 0)
+        lax.fori_loop(0, group - 1, post, 0)
         for way, present in enumerate((has_above, has_below)):
 
             @pl.when(present)
             def _():
                 for h in range(halo):
-                    stage(
-                        own,
-                        slab_ref[0, way * halo + h],
-                        send,
-                        send_slab_at + way * slab_span + h * kp,
-                    )
+                    values = rows_of(slab_ref[0, way * halo + h])
+                    for n in range(kp):
+                        send[send_slab_at + way * slab_span + h * kp + n] = values[n]
                 slab_copy(step, rem, way).start()
 
-        for s in range(peers):
-            stage(own, peer_ref[0, me * peers + s], rem, me * span + s * kp)
+    post_rows(0, lambda row: [own_a[row * kp + n] for n in range(kp)])
+
+    for step in range(3):
+        own, after = (own_a, own_b) if step % 2 == 0 else (own_b, own_a)
+        rem = rems[step]
+        for p in range(peers):
+            stage(own, peer_ref[0, me * peers + p], rem, me * span + p * kp)
 
         if step == 0:
             load_operator.wait()
@@ -165,8 +170,8 @@
             for n in range(kp):
                 value = None
                 for k in range(kl):
-                    match = match_ref[row, k * kp + n]
-                    at = jnp.where(match == kp, own_zero, local_ref[row, k] * kp + match)
+                    match = match_ref[k, n, row]
+                    at = jnp.where(match == kp, own_zero, local_ref[k, row] * kp + match)
                     term = jnp.dot(operator[row, k], own[at], preferred_element_type=jnp.float32)
                     value = term if value is None else value + term
                 local_sum[row * kp + n] = value
@@ -191,13 +196,13 @@
             def _():
                 slab_copy(step, rem, way).wait_recv()
 
-        def remote_row(row, carry):
+        def images_of(row):
             images = []
             for n in range(kp):
                 value = local_sum[row * kp + n]
                 for k in range(ko):
-                    match = match_ref[row, (kl + k) * kp + n]
-                    source = jnp.maximum(remote_ref[row, k] - rows, 0)
+                    match = match_ref[kl + k, n, row]
+                    source = jnp.maximum(remote_ref[k, row] - rows, 0)
                     from_below = (source >= group * peers) & (source < group * peers + halo)
                     from_above = source >= group * peers + halo
                     absent = (match == kp) | (from_below & (gx == 0)) | (from_above & (gx == slabs - 1))
@@ -206,27 +211,43 @@
                         operator[row, kl + k], rem[at], preferred_element_type=jnp.float32
                     )
                 images.append(value.astype(jnp.bfloat16))
-            if step < 2:
-                for n in range(kp):
-                    update = jnp.dot(diagonal[row], images[n], preferred_element_type=jnp.float32)
-                    before = own[row * kp + n].astype(jnp.float32)
-                    after[row * kp + n] = (before - update).astype(jnp.bfloat16)
-            else:
-                for n1 in range(kp):
-                    left = own[row * kp + n1]
-                    for n2 in range(kp):
-                        block = lax.dot_general(
-                            left,
-                            images[n2],
-                            (((0,), (0,)), ((), ())),
-                            preferred_element_type=jnp.float32,
-                        )
-                        partial[(row * kp + n1) * kp + n2] = block.astype(jnp.bfloat16)
-            return carry
-
-        lax.fori_loop(0, rows, remote_row, 0)
+            return images
+
+        def smoothed_row(row):
+            values = []
+            for n, image in enumerate(images_of(row)):
+                update = jnp.dot(diagonal[row], image, preferred_element_type=jnp.float32)
+                before = own[row * kp + n].astype(jnp.float32)
+                values.append((before - update).astype(jnp.bfloat16))
+            return values
+
+        def own_row(row, carry):
+            for n, value in enumerate(smoothed_row(row)):
+                after[row * kp + n] = value
+            return carry
+
+        def galerkin_row(row, carry):
+            images = images_of(row)
+            for n1 in range(kp):
+                left = own[row * kp + n1]
+                for n2 in range(kp):
+                    block = lax.dot_general(
+                        left,
+                        images[n2],
+                        (((0,), (0,)), ((), ())),
+                        preferred_element_type=jnp.float32,
+                    )
+                    partial[(row * kp + n1) * kp + n2] = block.astype(jnp.bfloat16)
+            return carry
+
+        if step < 2:
+            post_rows(step + 1, smoothed_row)
+            lax.fori_loop(0, rows, own_row, 0)
+        else:
+            lax.fori_loop(0, rows, galerkin_row, 0)
 
     core = me % 2
+    total_at = group * owned // 2
 
     def partner(step):
         def flip(bit):
@@ -242,7 +263,7 @@
 
     def half_copy(step, piece, length):
         at, count = pieces(length)[piece]
-        source = half_send.at[pl.ds(at, count)] if step == 0 else total.at[pl.ds(length + at, count)]
+        source = rem_a.at[pl.ds(at if step == 0 else total_at + length + at, count)]
         return pltpu.make_async_remote_copy(
             src_ref=source,
             dst_ref=landed[step].at[pl.ds(at, count)],
@@ -257,7 +278,7 @@
         at, count = pieces(length)[piece]
 
         def pick(j, carry):
-            half_send[at + j] = partial[inverse_ref[length + at + j]]
+            rem_a[at + j] = partial[inverse_ref[length + at + j]]
             return carry
 
         lax.fori_loop(0, count, pick, 0)
@@ -273,12 +294,12 @@
                 if step == 0:
                     mine = partial[inverse_ref[at + j]]
                 else:
-                    mine = total[at + j]
+                    mine = rem_a[total_at + at + j]
                 value = mine.astype(jnp.float32) + landed[step][at + j].astype(jnp.float32)
                 if last:
                     coarse_ref[at + j] = value.astype(jnp.bfloat16)
                 else:
-                    total[at + j] = value.astype(jnp.bfloat16)
+                    rem_a[total_at + at + j] = value.astype(jnp.bfloat16)
                 return carry
 
             lax.fori_loop(0, count, add, 0)
@@ -316,11 +337,12 @@
     count = rows * kp * kp
     dims = (slabs, group, rows, kl, ko, kp, peers, halo, owned)
 
-    slots = gather_order(lax.axis_index("gy"), group, owned)
-    named = coarse_slots.reshape(-1)
-    which = jnp.arange(count, dtype=jnp.int32) - count
+    named = coarse_slots.transpose(1, 2, 0)
+    slots = gather_order(lax.axis_index("gy"), group, owned, named.shape)
+    which = [lax.broadcasted_iota(jnp.int32, slots.shape, axis) for axis in (1, 2, 3)]
+    which = (which[2] * kp + which[0]) * kp + which[1] - count
     inverse = count + jnp.sum(
-        jnp.where(slots[:, None] == named[None, :], which[None, :], 0), axis=1, dtype=jnp.int32
+        jnp.where(slots == named[None], which, 0), axis=(1, 2, 3), dtype=jnp.int32
     )
 
     def blocks(n, dtype=jnp.bfloat16):
@@ -343,13 +365,12 @@
             blocks(rows),
             blocks(rows * kp + 1),
             blocks(rows * kp + 1),
+            blocks(max(remote_count + 1, 2 * half)),
             blocks(remote_count + 1),
             blocks(remote_count + 1),
             blocks(remote_count),
             blocks(rows * kp, jnp.float32),
             blocks(count + 1),
-            blocks(half),
-            blocks(half),
             *[blocks(half >> step) for step in range(bits)],
             pltpu.SemaphoreType.DMA((3,)),
             pltpu.SemaphoreType.DMA,
@@ -364,9 +385,9 @@
             collective_id=0, has_side_effects=True, vmem_limit_bytes=67_000_000
         ),
     )(
-        local_columns,
-        remote_columns,
-        match_slots.reshape(rows, -1),
+        local_columns.T,
+        remote_columns.T,
+        match_slots.transpose(1, 2, 0),
         peer_sends,
         slab_sends,
         inverse,

time: 136 us -> 125 us (0.919)
  Pallas kernels: 125 us -> 119 us
  local copies, waits for them, and re-layouts: 9.06 us -> 4.05 us
    pallas_call x1, Pallas kernels: 125 us -> 119 us  [body(): pl.pallas_call(functools.partial(kernel, dims), out_shape=(jax.ShapeDtype...]
    unnamed x7 -> x4, local copies, waits for them, and re-layouts: 7.51 us -> 4.05 us
    reshape x2 -> x0, local copies, waits for them, and re-layouts: 1.37 us -> none  [body(): match_slots.reshape(rows, -1)]
where the time goes in v2:
time: 125 us
  Pallas kernels  119 us (95%)
  local copies, waits for them, and re-layouts  4.05 us (3%)
  other arithmetic  1.32 us (1%)
    pallas_call x1, Pallas kernels, body(): pl.pallas_call(functools.partial(kernel, dims), out_shape=(jax.ShapeDtype...  119 us
    unnamed x4, local copies, waits for them, and re-layouts  4.05 us

profile of v2, /device:TPU:0, one launch (start us, length us, event | category | flops | bytes accessed | tf_op | source)
XLA Modules:
  0.0 125.1 jit_solution(4562758423531720924)
XLA Ops:
  0.7 0.8 select_reduce_fusion
  1.5 0.5 broadcast_add_fusion.inverse_ref
  2.0 119.0 %shard_map.104 = (bf16[16,256,256]{2,1,0:T(8,128)(2,1)}, bf16[6,256,256]{2,1,0:T(8,128)(2,1)}) custom-call(s32[2,8]{1,0:T(2,128)} %bitcast.11, s32[4,8]{1,0:T(4,128)} %bitcast.9, s32[6,2,8]{2,1,0:T(2,128)} %bitcast.8, s32[1,8]{1,0:T(1,128)} %peer_ref.1, s32[1,2]{1,0:T(1,128)} %slab_ref.1, s32[48]{0:T(128)} %broadcast_add_fusion.inverse_ref, ...), custom_call_target="tpu_custom_call" | custom-call | tf_op jit(solution)/shard_map/pallas_call | solution.py:355
  121.0 0.0 copy-start
  121.0 3.2 %copy.13 = bf16[8,2,256,256]{3,2,1,0:T(8,128)(2,1)} copy(bf16[8,2,256,256]{3,2,1,0:T(8,128)(2,1)} %bitcast.6) | data formatting | bytes 4194304
  124.2 0.0 copy-done
  124.2 0.9 copy.14
  (4 shorter events, 0.0 us)
Async XLA Ops:
  121.0 3.2 %copy-start = (bf16[6,256,256]{2,1,0:T(8,128)(2,1)S(1)}, bf16[6,256,256]{2,1,0:T(8,128)(2,1)}, u32[]{:S(2)}) copy-start(bf16[6,256,256]{2,1,0:T(8,128)(2,1)} %get-tuple-element.15) | copy-start | bytes 2359300

commit v3 on v2

--- a/solution.py
+++ b/solution.py
@@ -45,7 +45,7 @@
     rem_c,
     send,
     local_sum,
-    partial,
+    image,
     *rest,
 ):
     slabs, group, rows, kl, ko, kp, peers, halo, owned = dims
@@ -95,7 +95,7 @@
     rem_a[rem_zero] = zero
     rem_b[rem_zero] = zero
     rem_c[rem_zero] = zero
-    partial[rows * kp * kp] = zero
+    image[own_zero] = zero
     neighbours = jnp.where(has_below, 1, 0) + jnp.where(has_above, 1, 0)
     pl.semaphore_wait(barrier, group - 1 + neighbours)
 
@@ -226,25 +226,16 @@
                 after[row * kp + n] = value
             return carry
 
-        def galerkin_row(row, carry):
-            images = images_of(row)
-            for n1 in range(kp):
-                left = own[row * kp + n1]
-                for n2 in range(kp):
-                    block = lax.dot_general(
-                        left,
-                        images[n2],
-                        (((0,), (0,)), ((), ())),
-                        preferred_element_type=jnp.float32,
-                    )
-                    partial[(row * kp + n1) * kp + n2] = block.astype(jnp.bfloat16)
+        def image_row(row, carry):
+            for n, value in enumerate(images_of(row)):
+                image[row * kp + n] = value
             return carry
 
         if step < 2:
             post_rows(step + 1, smoothed_row)
             lax.fori_loop(0, rows, own_row, 0)
         else:
-            lax.fori_loop(0, rows, galerkin_row, 0)
+            lax.fori_loop(0, rows, image_row, 0)
 
     core = me % 2
     total_at = group * owned // 2
@@ -257,61 +248,70 @@
             return flip(1)
         return (1 - core) * flip(1 << step) + core * flip(1 << (bits - step))
 
-    def pieces(length):
-        middle = length // 2
-        return ((middle, length - middle), (0, middle))
-
-    def half_copy(step, piece, length):
-        at, count = pieces(length)[piece]
-        source = rem_a.at[pl.ds(at if step == 0 else total_at + length + at, count)]
+    grain = owned // 2 if owned % 2 == 0 else owned
+    half = group * owned // 2
+
+    def partial_at(place):
+        named = inverse_ref[place]
+        block = lax.dot_general(
+            own_a[named // kp],
+            image[named // (kp * kp) * kp + named % kp],
+            (((0,), (0,)), ((), ())),
+            preferred_element_type=jnp.float32,
+        )
+        return block.astype(jnp.bfloat16)
+
+    def half_copy(step, chunk):
+        at = chunk * grain
+        source = at if step == 0 else total_at + (half >> step) + at
         return pltpu.make_async_remote_copy(
-            src_ref=source,
-            dst_ref=landed[step].at[pl.ds(at, count)],
-            send_sem=half_send_sem.at[step, piece],
-            recv_sem=half_recv_sem.at[step, piece],
+            src_ref=rem_a.at[pl.ds(source, grain)],
+            dst_ref=landed[step].at[pl.ds(at, grain)],
+            send_sem=half_send_sem.at[step, chunk],
+            recv_sem=half_recv_sem.at[step, chunk],
             device_id=(gx, partner(step)),
             device_id_type=MESH,
         )
 
-    length = group * owned // 2
-    for piece in range(2):
-        at, count = pieces(length)[piece]
-
-        def pick(j, carry):
-            rem_a[at + j] = partial[inverse_ref[length + at + j]]
-            return carry
-
-        lax.fori_loop(0, count, pick, 0)
-        half_copy(0, piece, length).start()
-
+    def send_chunk(chunk):
+        def fill(j, carry):
+            rem_a[chunk * grain + j] = partial_at(half + chunk * grain + j)
+            return carry
+
+        lax.fori_loop(0, grain, fill, 0)
+        half_copy(0, chunk).start()
+
+    def add_chunk(step, chunk):
+        last = step == bits - 1
+        chunks = (half >> step) // grain
+        half_copy(step, chunk).wait_recv()
+
+        def add(j, carry):
+            at = chunk * grain + j
+            mine = partial_at(at) if step == 0 else rem_a[total_at + at]
+            value = mine.astype(jnp.float32) + landed[step][at].astype(jnp.float32)
+            if last:
+                coarse_ref[at] = value.astype(jnp.bfloat16)
+            else:
+                rem_a[total_at + at] = value.astype(jnp.bfloat16)
+            return carry
+
+        lax.fori_loop(0, grain, add, 0)
+        if not last and chunk >= chunks // 2:
+            half_copy(step + 1, chunk - chunks // 2).start()
+
+    chunks = half // grain
+    for chunk in reversed(range(chunks)):
+        send_chunk(chunk)
+        if chunk + 1 < chunks:
+            add_chunk(0, chunk + 1)
+    add_chunk(0, 0)
+    for step in range(1, bits):
+        for chunk in reversed(range((half >> step) // grain)):
+            add_chunk(step, chunk)
     for step in range(bits):
-        last = step == bits - 1
-        for piece in range(2):
-            at, count = pieces(length)[piece]
-            half_copy(step, piece, length).wait_recv()
-
-            def add(j, carry):
-                if step == 0:
-                    mine = partial[inverse_ref[at + j]]
-                else:
-                    mine = rem_a[total_at + at + j]
-                value = mine.astype(jnp.float32) + landed[step][at + j].astype(jnp.float32)
-                if last:
-                    coarse_ref[at + j] = value.astype(jnp.bfloat16)
-                else:
-                    rem_a[total_at + at + j] = value.astype(jnp.bfloat16)
-                return carry
-
-            lax.fori_loop(0, count, add, 0)
-            if piece == 0 and not last:
-                for sub in range(2):
-                    half_copy(step + 1, sub, length // 2).start()
-        length //= 2
-    length = group * owned // 2
-    for step in range(bits):
-        for piece in range(2):
-            half_copy(step, piece, length).wait_send()
-        length //= 2
+        for chunk in range((half >> step) // grain):
+            half_copy(step, chunk).wait_send()
     store_rows.wait()
 
 
@@ -370,7 +370,7 @@
             blocks(remote_count + 1),
             blocks(remote_count),
             blocks(rows * kp, jnp.float32),
-            blocks(count + 1),
+            blocks(rows * kp + 1),
             *[blocks(half >> step) for step in range(bits)],
             pltpu.SemaphoreType.DMA((3,)),
             pltpu.SemaphoreType.DMA,
@@ -378,8 +378,8 @@
             pltpu.SemaphoreType.DMA((3, group)),
             pltpu.SemaphoreType.DMA((3, 2)),
             pltpu.SemaphoreType.DMA((3, 2)),
-            pltpu.SemaphoreType.DMA((bits, 2)),
-            pltpu.SemaphoreType.DMA((bits, 2)),
+            pltpu.SemaphoreType.DMA((bits, group)),
+            pltpu.SemaphoreType.DMA((bits, group)),
         ],
         compiler_params=pltpu.CompilerParams(
             collective_id=0, has_side_effects=True, vmem_limit_bytes=67_000_000

time: 125 us -> 123 us (0.984)
  Pallas kernels: 119 us -> 116 us
    pallas_call x1, Pallas kernels: 119 us -> 116 us  [body(): pl.pallas_call(functools.partial(kernel, dims), out_shape=(jax.ShapeDtype...]
where the time goes in v3:
time: 123 us; the launch traced here: 122 us
  Pallas kernels  116 us (94%)
  local copies, waits for them, and re-layouts  4.05 us (3%)
  other arithmetic  1.32 us (1%)
    pallas_call x1, Pallas kernels, body(): pl.pallas_call(functools.partial(kernel, dims), out_shape=(jax.ShapeDtype...  116 us
    unnamed x4, local copies, waits for them, and re-layouts  4.05 us

profile of v3, /device:TPU:0, one launch (start us, length us, event | category | flops | bytes accessed | tf_op | source)
XLA Modules:
  0.0 122.3 jit_solution(15229581540633517843)
XLA Ops:
  0.7 0.8 select_reduce_fusion
  1.5 0.5 broadcast_add_fusion.inverse_ref
  2.0 116.3 %shard_map.104 = (bf16[16,256,256]{2,1,0:T(8,128)(2,1)}, bf16[6,256,256]{2,1,0:T(8,128)(2,1)}) custom-call(s32[2,8]{1,0:T(2,128)} %bitcast.11, s32[4,8]{1,0:T(4,128)} %bitcast.9, s32[6,2,8]{2,1,0:T(2,128)} %bitcast.8, s32[1,8]{1,0:T(1,128)} %peer_ref.1, s32[1,2]{1,0:T(1,128)} %slab_ref.1, s32[48]{0:T(128)} %broadcast_add_fusion.inverse_ref, ...), custom_call_target="tpu_custom_call" | custom-call | tf_op jit(solution)/shard_map/pallas_call | solution.py:355
  118.3 0.0 copy-start
  118.3 3.2 %copy.13 = bf16[8,2,256,256]{3,2,1,0:T(8,128)(2,1)} copy(bf16[8,2,256,256]{3,2,1,0:T(8,128)(2,1)} %bitcast.6) | data formatting | bytes 4194304
  121.5 0.0 copy-done
  121.5 0.9 copy.14
  (4 shorter events, 0.0 us)
Async XLA Ops:
  118.3 3.2 %copy-start = (bf16[6,256,256]{2,1,0:T(8,128)(2,1)S(1)}, bf16[6,256,256]{2,1,0:T(8,128)(2,1)}, u32[]{:S(2)}) copy-start(bf16[6,256,256]{2,1,0:T(8,128)(2,1)} %get-tuple-element.15) | copy-start | bytes 2359300
